TPU v7x, 32 devices: a whole 2x2x4 slice. The times are simulated.
32 devices in a mesh: grp: 2 (over y), chan: 4 (over z), day: 2 (over x), seg: 2 (over core).
Axes of the slice: x: 2, y: 2, z: 4, core: 2. Of those that a mesh axis runs over, the one named last changes fastest.
Arguments:
- records: bfloat16 [4, 4, 512, 2048], P('day', 'seg', ('grp', 'chan')), parts along dimension 2, may hold values from -30 to 30
- visits: int32 [3, 2, 512], P(None, None, ('grp', 'chan')), parts along dimension 2, may hold values from 0 to 63
Outputs:
- correlation: bfloat16 [256, 3, 2, 512], P(('day', 'seg'), None, None, ('grp', 'chan')), parts along dimension 3
There are 2 independent parts, one for each index of `grp`. A program takes and returns all parts, laid end to end along the dimension named above; each array names one. Nothing has to cross between parts.
All inputs are finite; a program needn't handle non-finite values.
Results may differ from a plain program's by a relative error of at most 0.0068.
Values may be sent and summed in bfloat16 or wider, within the bound.
No kernel may reach another device: no remote copies, remote signals or barrier semaphores. Data moves between devices by JAX's collectives and lax.ppermute only.
A program may use at most 64 MiB of HBM per device.

v0:
```python
import functools
import math

import jax
import jax.numpy as jnp
import numpy as np
from jax import lax
from jax.experimental import pallas as pl
from jax.experimental.pallas import tpu as pltpu
from jax.sharding import PartitionSpec as P


NS = 2048
FREQS = 512
BAND = 64
LAGS = 256
SEGS = 4
FOLD = 4
SPAN = NS // FOLD
CLASS = FREQS // FOLD
PAIR = 2 * CLASS
WIDTH = 2 * FREQS
GRANT = 24 << 20
BF16 = jnp.bfloat16
F32 = jnp.float32


def trig_columns(index):
    blocks = []
    for r in range(FOLD):
        freqs = FOLD * np.arange(CLASS) + r
        turns = (index[:, None] * freqs[None, :] % NS) * (2.0 * math.pi / NS)
        blocks += [np.cos(turns), -np.sin(turns)]
    return np.concatenate(blocks, 1).astype(jnp.bfloat16)


def in_vmem():
    return pl.BlockSpec(memory_space=pltpu.VMEM)


def cost(flops, ops):
    size = sum(int(np.prod(op.shape)) * op.dtype.itemsize for op in ops)
    return pl.CostEstimate(flops=flops, bytes_accessed=size, transcendentals=0)


def call(kernel, ops, out_shape, flops, scratch=(), hbm=0):
    ops = [pltpu.with_memory_space_constraint(op, pltpu.HBM) for op in ops[:hbm]] + ops[hbm:]
    return pl.pallas_call(
        kernel,
        out_shape=out_shape,
        in_specs=[pl.BlockSpec(memory_space=pltpu.HBM)] * hbm + [in_vmem() for _ in ops[hbm:]],
        out_specs=jax.tree.map(lambda s: in_vmem(), out_shape),
        scratch_shapes=list(scratch),
        cost_estimate=cost(flops, ops),
        compiler_params=pltpu.CompilerParams(vmem_limit_bytes=GRANT),
    )(*ops)


def shape(dims, dtype=BF16):
    return jax.ShapeDtypeStruct(dims, dtype)


def whiten(x, t_ref, out_ref):
    rows = x.shape[0]
    stacked = jnp.concatenate([x[:, q * SPAN : (q + 1) * SPAN] for q in range(FOLD)], 0)
    spec = []
    power = None
    for r in range(FOLD):
        product = jnp.dot(stacked, t_ref[r], preferred_element_type=F32)
        p = [product[q * rows : (q + 1) * rows] for q in range(FOLD)]
        if r % 2 == 0:
            even, odd = p[0] + p[2], p[1] + p[3]
            both = even + odd if r == 0 else even - odd
            real, imag = both[:, :CLASS], both[:, CLASS:]
        else:
            even, odd = p[0] - p[2], p[1] - p[3]
            if r == 1:
                real = even[:, :CLASS] + odd[:, CLASS:]
                imag = even[:, CLASS:] - odd[:, :CLASS]
            else:
                real = even[:, :CLASS] - odd[:, CLASS:]
                imag = even[:, CLASS:] + odd[:, :CLASS]
        square = real * real + imag * imag
        power = square if power is None else power + square
        spec.append((real, imag))
    group = BAND // FOLD
    same = (
        lax.broadcasted_iota(jnp.int32, (CLASS, CLASS), 0) // group
        == lax.broadcasted_iota(jnp.int32, (CLASS, CLASS), 1) // group
    )
    ones = jnp.where(same, 1.0, 0.0).astype(BF16)
    high = power.astype(BF16)
    low = (power - high.astype(F32)).astype(BF16)
    total = jnp.dot(high, ones, preferred_element_type=F32) + jnp.dot(
        low, ones, preferred_element_type=F32
    )
    factor = lax.rsqrt(total * (0.5 / BAND) + 1e-06)
    for r, (real, imag) in enumerate(spec):
        out_ref[:, r * PAIR : r * PAIR + CLASS] = (real * factor).astype(BF16)
        out_ref[:, r * PAIR + CLASS : (r + 1) * PAIR] = (imag * factor).astype(BF16)


def first_kernel(x_hbm, t_hbm, vis_hbm, out_ref, t_ref, vis_ref, x_ref, sem):
    copies = [
        pltpu.make_async_copy(x_hbm.at[0, 0], x_ref, sem.at[0]),
        pltpu.make_async_copy(t_hbm, t_ref, sem.at[1]),
        pltpu.make_async_copy(vis_hbm, vis_ref, sem.at[2]),
    ]
    for copy in copies:
        copy.start()
    for copy in copies:
        copy.wait()
    whiten(x_ref[...], t_ref, out_ref)


def second_kernel(first, count, x_hbm, t_ref, out_ref, rest_ref, x_ref, sem):
    segs, chans = x_hbm.shape[1], x_hbm.shape[2]
    copies = []
    for n in range(x_hbm.shape[0] * segs - first):
        target = x_ref.at[n] if n < count else rest_ref.at[n - count]
        unit = first + n
        copies.append(pltpu.make_async_copy(x_hbm.at[unit // segs, unit % segs], target, sem.at[n]))
    for copy in copies:
        copy.start()
    for copy in copies[:count]:
        copy.wait()
    whiten(x_ref[...].reshape(count * chans, NS), t_ref, out_ref)
    for copy in copies[count:]:
        copy.wait()


def later_kernel(x_ref, t_ref, out_ref):
    whiten(x_ref[...].reshape(out_ref.shape[0], NS), t_ref, out_ref)


def spectra_chunks(records, table, visits):
    days, segs, chans, _ = records.shape
    units = days * segs
    flops = 2 * chans * NS * WIDTH
    first, table, visits = call(
        first_kernel,
        [records, table, visits],
        (shape((chans, WIDTH)), shape(table.shape), shape(visits.shape, visits.dtype)),
        flops,
        [pltpu.VMEM((chans, NS), BF16), pltpu.SemaphoreType.DMA((3,))],
        hbm=3,
    )
    chunks = [first]
    count = max(units - 2, 1)
    left = units - 1 - count
    if units > 1:
        chunk, rest = call(
            functools.partial(second_kernel, 1, count),
            [records, table],
            (shape((count * chans, WIDTH)), shape((max(left, 1), chans, NS))),
            count * flops,
            [pltpu.VMEM((count, chans, NS), BF16), pltpu.SemaphoreType.DMA((units - 1,))],
            hbm=1,
        )
        chunks.append(chunk)
    if left:
        chunks.append(call(later_kernel, [rest, table], shape((left * chans, WIDTH)), left * flops))
    return chunks, visits


def one_hot(block, chans):
    row = jnp.concatenate([block[p : p + 1, :] for p in range(block.shape[0])], 1).astype(F32)
    chosen = lax.broadcasted_iota(jnp.int32, (chans, row.shape[1]), 0).astype(F32) == row
    return jnp.where(chosen, 1.0, 0.0).astype(F32).T.astype(BF16)


def cross_block(receivers, sources, select, r):
    cols = slice(r * PAIR, (r + 1) * PAIR)
    picks = select.shape[0] // receivers[0].shape[0]
    real = imag = None
    for own, other in zip(receivers, sources):
        g = jnp.dot(select, other[:, cols], preferred_element_type=F32)
        u = own[:, cols].astype(F32)
        u = jnp.concatenate([u] * picks, 0)
        ur, ui, gr, gi = u[:, :CLASS], u[:, CLASS:], g[:, :CLASS], g[:, CLASS:]
        a = ur * gr + ui * gi
        b = ur * gi - ui * gr
        real = a if real is None else real + a
        imag = b if imag is None else imag + b
    return jnp.concatenate([real, imag], 1).astype(BF16)


def lag_terms(inv_ref, receivers, sources, select):
    total = None
    for r in range(FOLD):
        block = cross_block(receivers, sources, select, r)
        part = lax.dot_general(
            inv_ref[:, r * PAIR : (r + 1) * PAIR],
            block,
            (((1,), (1,)), ((), ())),
            preferred_element_type=F32,
        )
        total = part if total is None else total + part
    return total


def units_of(ref, chans):
    return [ref.at[n * chans : (n + 1) * chans, :] for n in range(ref.shape[0] // chans)]


def center_kernel(inv_ref, vis_ref, *refs):
    chunks, out_ref, select_ref = refs[:-2], refs[-2], refs[-1]
    chans = vis_ref.shape[2]
    reach = vis_ref.shape[0] // 2
    units = [u for ref in chunks for u in units_of(ref, chans)]
    for n in range(reach):
        select_ref[n] = one_hot(vis_ref[reach + 1 + n], chans)
    out_ref[...] = lag_terms(inv_ref, units, units, one_hot(vis_ref[reach], chans))


def select_kernel(wanted, *refs):
    out_ref = refs[-1]
    for n, (which, visit) in enumerate(wanted):
        out_ref[n] = one_hot(refs[which][visit], refs[which].shape[2])


def pair_terms(jobs, inv_ref, selects, blocks):
    chans = selects[0].shape[2]
    units = [units_of(ref, chans) for ref in blocks]
    return [
        lag_terms(inv_ref, units[receiver], units[source], selects[which][index])
        for receiver, source, which, index in jobs
    ]


def pair_kernel(jobs, n_blocks, inv_ref, near_ref, far_ref, *refs):
    blocks, out_ref = refs[:n_blocks], refs[-1]
    wide = near_ref.shape[1]
    for n, value in enumerate(pair_terms(jobs, inv_ref, (near_ref, far_ref), blocks)):
        cols = slice(n * wide, (n + 1) * wide)
        if len(refs) > n_blocks + 1:
            value = value + refs[n_blocks][:, cols]
        out_ref[:, cols] = value


def split_kernel(share, n_day, n_seg, n_parts, *refs):
    parts, keep_ref, send_ref = refs[:n_parts], refs[-2], refs[-1]
    day, seg = lax.axis_index("day"), lax.axis_index("seg")
    for ds in range(n_seg):
        for dd in range(n_day):
            block = lax.rem(day + dd, n_day) * n_seg + lax.rem(seg + ds, n_seg)
            rows = pl.ds(pl.multiple_of(block * share, share), share)
            at = 0
            for ref in parts:
                value = ref[rows, :]
                cols = slice(at, at + ref.shape[1])
                if ds == 0:
                    keep_ref[dd * share : (dd + 1) * share, cols] = value
                else:
                    send_ref[ds - 1, dd * share : (dd + 1) * share, cols] = value.astype(BF16)
                at += ref.shape[1]


def last_pair_kernel(pair_args, split_args, n_in, *refs):
    ins, parts, (keep_ref, send_ref, total) = refs[:n_in], refs[n_in:-3], refs[-3:]
    pair_kernel(*pair_args, *ins, total)
    split_kernel(*split_args, *parts, total, keep_ref, send_ref)


def merge_kernel(share, wide, groups, n_got, *refs):
    keep_ref, got, outs = refs[0], refs[1 : 1 + n_got], refs[1 + n_got :]
    n_day = keep_ref.shape[0] // share
    for dd in range(n_day):
        rows = slice(dd * share, (dd + 1) * share)
        for g, group in enumerate(groups):
            for place, n in enumerate(group):
                cols = slice(n * wide, (n + 1) * wide)
                value = keep_ref[rows, cols]
                for ref in got:
                    value = value + ref[rows, cols].astype(F32)
                to = slice(place * wide, (place + 1) * wide)
                if g == 0 and dd == 0:
                    outs[0][:, to] = value
                elif g == 0:
                    outs[1][dd - 1, :, to] = value.astype(BF16)
                else:
                    outs[g + 1][dd, :, to] = value.astype(BF16)


def line_plan(n_chan):
    up = [(i, i + 1) for i in range(n_chan - 1)]
    back = [(i + 1, i) for i in range(n_chan - 1)]
    arrivals = [up, [(n_chan - 1, 1)]]
    wanted = [(0, 0), (0, 2), (1, 0)]
    jobs = [(0, 1, 0, 0), (1, 0, 1, 0), (1, 2, 1, 1), (2, 1, 1, 2)]
    visits_of = [2, 0, 2, 0]
    ways = [None, 0, 0, 1]
    routes = [back, [(1, n_chan - 1)]]
    return [(arrivals, wanted, jobs, visits_of, ways)], routes


def ring_plan(n_chan, reach):
    groups, routes = [], []
    for o in range(1, reach + 1):
        to = [(i, (i + o) % n_chan) for i in range(n_chan)]
        routes.append([(j, i) for i, j in to])
        jobs = [(0, 1, 0, o - 1), (1, 0, 1, 0)]
        groups.append(([to], [(0, reach - o)], jobs, [reach + o, reach - o], [None, o - 1]))
    return groups, routes


def local(records, visits):
    day_local, _, chans, _ = records.shape
    visit_count, picks, _ = visits.shape
    reach = visit_count // 2
    n_chan, n_day, n_seg = (lax.axis_size(a) for a in ("chan", "day", "seg"))
    share = LAGS // (n_day * n_seg)
    wide = picks * chans
    table = trig_columns(np.arange(SPAN)).reshape(SPAN, FOLD, PAIR).transpose(1, 0, 2)
    table = jnp.asarray(np.ascontiguousarray(table))
    inverse = jnp.asarray(trig_columns(np.arange(LAGS) - LAGS // 2))
    line = reach == 1 and n_chan > 2
    plan, routes = line_plan(n_chan) if line else ring_plan(n_chan, reach)

    chunks, visits = spectra_chunks(records, table, visits)
    held, asked = [], []
    for arrivals, *_ in plan:
        held.append([[lax.ppermute(c, "chan", to) for to in arrivals] for c in chunks])
        asked.append([lax.ppermute(visits, "chan", to) for to in arrivals])

    flops = 2 * wide * LAGS * WIDTH
    center, near = call(
        center_kernel,
        [inverse, visits, *chunks],
        (shape((LAGS, wide), F32), shape((reach, wide, chans))),
        flops,
    )
    parts = [center]
    visit_of, way_of = [reach], [None]
    for g, (arrivals, wanted, jobs, visits_of, ways) in enumerate(plan):
        visit_of += visits_of
        way_of += ways
        far = call(
            functools.partial(select_kernel, wanted), asked[g], shape((len(wanted), wide, chans)), 0
        )
        total = None
        for n, chunk in enumerate(chunks):
            args = (jobs, 1 + len(arrivals))
            ops = [inverse, near, far, chunk, *held[g][n]] + ([] if total is None else [total])
            if g == len(plan) - 1 and n == len(chunks) - 1:
                cols = len(visit_of) * wide
                keep, send = call(
                    functools.partial(
                        last_pair_kernel, args, (share, n_day, n_seg, len(parts) + 1), len(ops)
                    ),
                    ops + parts,
                    (
                        shape((n_day * share, cols), F32),
                        shape((n_seg - 1, n_day * share, cols)),
                    ),
                    len(jobs) * flops,
                    [pltpu.VMEM((LAGS, len(jobs) * wide), F32)],
                )
            else:
                total = call(
                    functools.partial(pair_kernel, *args),
                    ops,
                    shape((LAGS, len(jobs) * wide), F32),
                    len(jobs) * flops,
                )
        parts.append(total)

    got = []
    for ds in range(1, n_seg):
        route = [(i, (i + ds) % n_seg) for i in range(n_seg)]
        got.append(lax.ppermute(send[ds - 1], "seg", route))
    groups = [[n for n, way in enumerate(way_of) if way is None]]
    groups += [[n for n, way in enumerate(way_of) if way == k] for k in range(len(routes))]
    own, by_day, *away = call(
        functools.partial(merge_kernel, share, wide, groups, len(got)),
        [keep, *got],
        (
            shape((share, len(groups[0]) * wide), F32),
            shape((max(n_day - 1, 1), share, len(groups[0]) * wide)),
            *[shape((n_day, share, len(g) * wide)) for g in groups[1:]],
        ),
        0,
    )
    columns = [None] * visit_count

    def add(group, values):
        for place, n in enumerate(group):
            v = visit_of[n]
            value = values[:, place * wide : (place + 1) * wide].astype(F32)
            columns[v] = value if columns[v] is None else columns[v] + value

    for k, pairs in enumerate(routes):
        for dd in range(n_day):
            route = [
                (i * n_day + d, j * n_day + (d + dd) % n_day) for i, j in pairs for d in range(n_day)
            ]
            add(groups[k + 1], lax.ppermute(away[k][dd], ("chan", "day"), route))
    for dd in range(1, n_day):
        route = [(i, (i + dd) % n_day) for i in range(n_day)]
        add(groups[0], lax.ppermute(by_day[dd - 1], "day", route))
    add(groups[0], own)
    days_all = day_local * n_day
    scale = 1.0 / math.sqrt(FREQS * days_all * SEGS)
    result = (jnp.concatenate(columns, 1) * scale).astype(BF16)
    return result.reshape(share, visit_count, picks, chans)


def solution(mesh):
    in_specs = (P("day", "seg", ("grp", "chan"), None), P(None, None, ("grp", "chan")))
    out_specs = P(("day", "seg"), None, None, ("grp", "chan"))

    return jax.shard_map(local, mesh=mesh, in_specs=in_specs, out_specs=out_specs, check_vma=False)
```

profile of v0, /device:TPU:24, one launch (start us, length us, event | category | flops | bytes accessed | tf_op | source)
XLA Modules:
  0.0 54.4 jit_solution(14574178026289638840)
XLA Ops:
  0.0 1.9 %shard_map.46 = (bf16[64,1024]{1,0:T(8,128)(2,1)S(1)}, bf16[4,512,256]{2,1,0:T(8,128)(2,1)S(1)}, s32[3,2,64]{2,1,0:T(2,128)S(1)}) custom-call(bf16[2,2,64,2048]{3,2,1,0:T(8,128)(2,1)} %x_hbm.3, bf16[4,512,256]{2,1,0:T(8,128)(2,1)} %constant.6.clone.t_hbm, s32[3,2,64]{2,1,0:T(2,128)} %vis_hbm.1), custom_call_target="tpu_custom_call" | custom-call | flops 268435456 | bytes 2098688 | tf_op jit(solution)/shard_map/pallas_call | solution.py:48
  1.9 1.9 %shard_map.47 = (bf16[128,1024]{1,0:T(8,128)(2,1)S(1)}, bf16[1,64,2048]{2,1,0:T(8,128)(2,1)S(1)}) custom-call(bf16[2,2,64,2048]{3,2,1,0:T(8,128)(2,1)} %x_hbm.3, bf16[4,512,256]{2,1,0:T(8,128)(2,1)S(1)} %get-tuple-element.20.t_ref), custom_call_target="tpu_custom_call" | custom-call | flops 536870912 | bytes 2097152 | tf_op jit(solution)/shard_map/pallas_call | solution.py:48
  3.9 1.3 %collective-permute-start.4 = (bf16[128,1024]{1,0:T(8,128)(2,1)S(1)}, bf16[128,1024]{1,0:T(8,128)(2,1)S(1)}, u32[]{:S(2)}, u32[]{:S(2)}) collective-permute-start(bf16[128,1024]{1,0:T(8,128)(2,1)S(1)} %get-tuple-element.21.refs_1_.refs_0_), channel_id=1, source_target_pairs={{0,4},{4,8},{8,12},{1,5},{5,9},{9,13},{2,6},{6,10},{10,14},{3,7},{... | collective-permute-start | bytes 786440 | tf_op jit(solution)/shard_map/ppermute | solution.py:323
  5.2 4.4 %collective-permute-start.5 = (bf16[128,1024]{1,0:T(8,128)(2,1)S(1)}, bf16[128,1024]{1,0:T(8,128)(2,1)S(1)}, u32[]{:S(2)}, u32[]{:S(2)}) collective-permute-start(bf16[128,1024]{1,0:T(8,128)(2,1)S(1)} %get-tuple-element.21.refs_1_.refs_0_), channel_id=1, source_target_pairs={{12,4},{13,5},{14,6},{15,7},{28,20},{29,21},{30,22},{31,23}} | collective-permute-start | bytes 786440 | tf_op jit(solution)/shard_map/ppermute | solution.py:323
  9.6 1.3 %collective-permute-start.6 = (bf16[64,1024]{1,0:T(8,128)(2,1)S(1)}, bf16[64,1024]{1,0:T(8,128)(2,1)S(1)}, u32[]{:S(2)}, u32[]{:S(2)}) collective-permute-start(bf16[64,1024]{1,0:T(8,128)(2,1)S(1)} %get-tuple-element.19.refs_0_), channel_id=1, source_target_pairs={{0,4},{4,8},{8,12},{1,5},{5,9},{9,13},{2,6},{6,10},{10,14},{3,7},{... | collective-permute-start | bytes 393224 | tf_op jit(solution)/shard_map/ppermute | solution.py:323
  10.9 2.9 %collective-permute-start.7 = (bf16[64,1024]{1,0:T(8,128)(2,1)S(1)}, bf16[64,1024]{1,0:T(8,128)(2,1)S(1)}, u32[]{:S(2)}, u32[]{:S(2)}) collective-permute-start(bf16[64,1024]{1,0:T(8,128)(2,1)S(1)} %get-tuple-element.19.refs_0_), channel_id=1, source_target_pairs={{12,4},{13,5},{14,6},{15,7},{28,20},{29,21},{30,22},{31,23}} | collective-permute-start | bytes 393224 | tf_op jit(solution)/shard_map/ppermute | solution.py:323
  13.8 1.3 %collective-permute-start = (s32[3,2,64]{2,1,0:T(2,128)S(1)}, s32[3,2,64]{2,1,0:T(2,128)S(1)}, u32[]{:S(2)}, u32[]{:S(2)}) collective-permute-start(s32[3,2,64]{2,1,0:T(2,128)S(1)} %get-tuple-element.18.vis_ref), channel_id=1, source_target_pairs={{0,4},{4,8},{8,12},{1,5},{5,9},{9,13},{2,6},{6,10},{10,14},{3,7},{... | collective-permute-start | bytes 4616 | tf_op jit(solution)/shard_map/ppermute | solution.py:324
  15.1 4.2 %collective-permute-done.refs_0_ = s32[3,2,64]{2,1,0:T(2,128)S(1)} collective-permute-done((s32[3,2,64]{2,1,0:T(2,128)S(1)}, s32[3,2,64]{2,1,0:T(2,128)S(1)}, u32[]{:S(2)}, u32[]{:S(2)}) %collective-permute-start) | collective-permute-done | bytes 1568 | tf_op jit(solution)/shard_map/ppermute | solution.py:324
  19.3 1.5 %collective-permute-start.1 = (s32[3,2,64]{2,1,0:T(2,128)S(1)}, s32[3,2,64]{2,1,0:T(2,128)S(1)}, u32[]{:S(2)}, u32[]{:S(2)}) collective-permute-start(s32[3,2,64]{2,1,0:T(2,128)S(1)} %get-tuple-element.18.vis_ref), channel_id=1, source_target_pairs={{12,4},{13,5},{14,6},{15,7},{28,20},{29,21},{30,22},{31,23}} | collective-permute-start | bytes 4616 | tf_op jit(solution)/shard_map/ppermute | solution.py:324
  20.8 0.0 copy-start
  20.9 0.6 %shard_map.48.refs_2_.refs_3_ = bf16[64,1024]{1,0:T(8,128)(2,1)S(1)} custom-call(bf16[1,64,2048]{2,1,0:T(8,128)(2,1)S(1)} %get-tuple-element.22.x_ref, bf16[4,512,256]{2,1,0:T(8,128)(2,1)S(1)} %get-tuple-element.20.t_ref), custom_call_target="tpu_custom_call" | custom-call | flops 268435456 | bytes 1310720 | tf_op jit(solution)/shard_map/pallas_call | solution.py:48
  21.4 0.7 %collective-permute-done.1.refs_1_ = s32[3,2,64]{2,1,0:T(2,128)S(1)} collective-permute-done((s32[3,2,64]{2,1,0:T(2,128)S(1)}, s32[3,2,64]{2,1,0:T(2,128)S(1)}, u32[]{:S(2)}, u32[]{:S(2)}) %collective-permute-start.1) | collective-permute-done | bytes 1568 | tf_op jit(solution)/shard_map/ppermute | solution.py:324
  22.1 1.3 %collective-permute-start.2 = (bf16[64,1024]{1,0:T(8,128)(2,1)S(1)}, bf16[64,1024]{1,0:T(8,128)(2,1)S(1)}, u32[]{:S(2)}, u32[]{:S(2)}) collective-permute-start(bf16[64,1024]{1,0:T(8,128)(2,1)S(1)} %shard_map.48.refs_2_.refs_3_), channel_id=1, source_target_pairs={{0,4},{4,8},{8,12},{1,5},{5,9},{9,13},{2,6},{6,10},{10,14},{3,7},{... | collective-permute-start | bytes 393224 | tf_op jit(solution)/shard_map/ppermute | solution.py:323
  23.4 5.7 %collective-permute-start.3 = (bf16[64,1024]{1,0:T(8,128)(2,1)S(1)}, bf16[64,1024]{1,0:T(8,128)(2,1)S(1)}, u32[]{:S(2)}, u32[]{:S(2)}) collective-permute-start(bf16[64,1024]{1,0:T(8,128)(2,1)S(1)} %shard_map.48.refs_2_.refs_3_), channel_id=1, source_target_pairs={{12,4},{13,5},{14,6},{15,7},{28,20},{29,21},{30,22},{31,23}} | collective-permute-start | bytes 393224 | tf_op jit(solution)/shard_map/ppermute | solution.py:323
  29.2 1.0 %shard_map.49 = (f32[256,128]{1,0:T(8,128)S(1)}, bf16[1,128,64]{2,1,0:T(8,128)(2,1)S(1)}) custom-call(bf16[256,1024]{1,0:T(8,128)(2,1)S(1)} %copy-done, s32[3,2,64]{2,1,0:T(2,128)S(1)} %get-tuple-element.18.vis_ref, bf16[64,1024]{1,0:T(8,128)(2,1)S(1)} %get-tuple-element.19.refs_0_, bf16[128,1024]{1,0:T(8,128)(2,1)S(1)} %get-tuple-element.21.refs_1_.refs_0_, ...), custom_call_target="tpu_custom_call" | custom-call | flops 67108864 | bytes 1050112 | tf_op jit(solution)/shard_map/pallas_call | solution.py:48
  30.2 0.2 shard_map.50.far_ref.refs_2_
  30.4 1.5 %shard_map.51.refs_3_ = f32[256,512]{1,0:T(8,128)S(1)} custom-call(bf16[256,1024]{1,0:T(8,128)(2,1)S(1)} %copy-done, bf16[1,128,64]{2,1,0:T(8,128)(2,1)S(1)} %get-tuple-element.23.near_ref.refs_1_, bf16[3,128,64]{2,1,0:T(8,128)(2,1)S(1)} %shard_map.50.far_ref.refs_2_, bf16[64,1024]{1,0:T(8,128)(2,1)S(1)} %get-tuple-element.19.refs_0_, ...), custom_call_target="tpu_custom_call" | custom-call | flops 268435456 | bytes 983040 | tf_op jit(solution)/shard_map/pallas_call | solution.py:48
  31.9 2.3 %shard_map.52.refs_6_ = f32[256,512]{1,0:T(8,128)S(1)} custom-call(bf16[256,1024]{1,0:T(8,128)(2,1)S(1)} %copy-done, bf16[1,128,64]{2,1,0:T(8,128)(2,1)S(1)} %get-tuple-element.23.near_ref.refs_1_, bf16[3,128,64]{2,1,0:T(8,128)(2,1)S(1)} %shard_map.50.far_ref.refs_2_, bf16[128,1024]{1,0:T(8,128)(2,1)S(1)} %get-tuple-element.21.refs_1_.refs_0_, ...), custom_call_target="tpu_custom_call" | custom-call | flops 268435456 | bytes 1900544 | tf_op jit(solution)/shard_map/pallas_call | solution.py:48
  34.2 2.1 %shard_map.53 = (f32[128,640]{1,0:T(8,128)S(1)}, bf16[1,128,640]{2,1,0:T(8,128)(2,1)S(1)}) custom-call(bf16[256,1024]{1,0:T(8,128)(2,1)S(1)} %copy-done, bf16[1,128,64]{2,1,0:T(8,128)(2,1)S(1)} %get-tuple-element.23.near_ref.refs_1_, bf16[3,128,64]{2,1,0:T(8,128)(2,1)S(1)} %shard_map.50.far_ref.refs_2_, bf16[64,1024]{1,0:T(8,128)(2,1)S(1)} %shard_map.48.refs_2_.refs_3_, ...), custom_call_target="tpu_custom_call" | custom-call | flops 268435456 | bytes 1638400 | tf_op jit(solution)/shard_map/pallas_call | solution.py:48
  36.3 0.1 collective-permute-start.8
  36.4 1.4 %collective-permute-done.8.refs_1_ = bf16[128,640]{1,0:T(8,128)(2,1)S(1)} collective-permute-done((bf16[128,640]{1,0:T(8,128)(2,1)S(1)}, bf16[128,640]{1,0:T(8,128)(2,1)S(1)}, u32[]{:S(2)}, u32[]{:S(2)}) %collective-permute-start.8) | collective-permute-done | bytes 163872 | tf_op jit(solution)/shard_map/ppermute | solution.py:371
  37.8 1.3 %collective-permute-start.10 = (bf16[64,256]{1,0:T(8,128)(2,1)S(1)}, bf16[64,256]{1,0:T(8,128)(2,1)S(1)}, u32[]{:S(2)}, u32[]{:S(2)}) collective-permute-start(bf16[64,256]{1,0:T(8,128)(2,1)S(1)} %get-tuple-element.35), channel_id=1, source_target_pairs={{4,2},{6,0},{8,6},{10,4},{12,10},{14,8},{5,3},{7,1},{9,7},{11,5},{... | collective-permute-start | bytes 98312 | tf_op jit(solution)/shard_map/ppermute | solution.py:397
  39.1 4.8 %collective-permute-start.9 = (bf16[64,256]{1,0:T(8,128)(2,1)S(1)}, bf16[64,256]{1,0:T(8,128)(2,1)S(1)}, u32[]{:S(2)}, u32[]{:S(2)}) collective-permute-start(bf16[64,256]{1,0:T(8,128)(2,1)S(1)} %get-tuple-element.34), channel_id=1, source_target_pairs={{4,0},{6,2},{8,4},{10,6},{12,8},{14,10},{5,1},{7,3},{9,5},{11,7},{... | collective-permute-start | bytes 98312 | tf_op jit(solution)/shard_map/ppermute | solution.py:397
  43.9 0.6 %collective-permute-start.13 = (bf16[64,256]{1,0:T(8,128)(2,1)S(1)}, bf16[64,256]{1,0:T(8,128)(2,1)S(1)}, u32[]{:S(2)}, u32[]{:S(2)}) collective-permute-start(bf16[64,256]{1,0:T(8,128)(2,1)S(1)} %bitcast.14), channel_id=1, source_target_pairs={{0,2},{2,0},{1,3},{3,1},{4,6},{6,4},{5,7},{7,5},{8,10},{10,8},{9,1... | collective-permute-start | bytes 98312 | tf_op jit(solution)/shard_map/ppermute | solution.py:400
  44.6 1.3 %collective-permute-start.11 = (bf16[64,128]{1,0:T(8,128)(2,1)S(1)}, bf16[64,128]{1,0:T(8,128)(2,1)S(1)}, u32[]{:S(2)}, u32[]{:S(2)}) collective-permute-start(bf16[64,128]{1,0:T(8,128)(2,1)S(1)} %get-tuple-element.36), channel_id=1, source_target_pairs={{4,12},{6,14},{5,13},{7,15},{20,28},{22,30},{21,29},{23,31}} | collective-permute-start | bytes 49160 | tf_op jit(solution)/shard_map/ppermute | solution.py:397
  45.8 1.3 %collective-permute-start.12 = (bf16[64,128]{1,0:T(8,128)(2,1)S(1)}, bf16[64,128]{1,0:T(8,128)(2,1)S(1)}, u32[]{:S(2)}, u32[]{:S(2)}) collective-permute-start(bf16[64,128]{1,0:T(8,128)(2,1)S(1)} %get-tuple-element.37), channel_id=1, source_target_pairs={{4,14},{6,12},{5,15},{7,13},{20,30},{22,28},{21,31},{23,29}} | collective-permute-start | bytes 49160 | tf_op jit(solution)/shard_map/ppermute | solution.py:397
  47.1 3.9 %collective-permute-done.11 = bf16[64,128]{1,0:T(8,128)(2,1)S(1)} collective-permute-done((bf16[64,128]{1,0:T(8,128)(2,1)S(1)}, bf16[64,128]{1,0:T(8,128)(2,1)S(1)}, u32[]{:S(2)}, u32[]{:S(2)}) %collective-permute-start.11) | collective-permute-done | bytes 16416 | tf_op jit(solution)/shard_map/ppermute | solution.py:397
  51.1 2.2 %collective-permute-done.12 = bf16[64,128]{1,0:T(8,128)(2,1)S(1)} collective-permute-done((bf16[64,128]{1,0:T(8,128)(2,1)S(1)}, bf16[64,128]{1,0:T(8,128)(2,1)S(1)}, u32[]{:S(2)}, u32[]{:S(2)}) %collective-permute-start.12) | collective-permute-done | bytes 16416 | tf_op jit(solution)/shard_map/ppermute | solution.py:397
  53.3 0.1 concatenate.10
  53.4 0.1 concatenate.11
  53.5 0.1 concatenate.12
  53.7 0.8 %fusion = bf16[64,3,2,64]{3,2,1,0:T(2,128)(2,1)} fusion(f32[64,1,2,64]{3,2,1,0:T(2,128)S(1)} %bitcast.17, f32[64,1,2,64]{3,2,1,0:T(2,128)S(1)} %bitcast.16, f32[64,1,2,64]{3,2,1,0:T(2,128)S(1)} %bitcast.15), kind=kLoop, calls=%fused_computation.1 | loop fusion | flops 98304 | bytes 147456 | tf_op jit(solution)/shard_map/convert_element_type | solution.py:404
  (14 shorter events, 0.1 us)
Async XLA Ops:
  3.9 28.0 %collective-permute-start.4 = (bf16[128,1024]{1,0:T(8,128)(2,1)S(1)}, bf16[128,1024]{1,0:T(8,128)(2,1)S(1)}, u32[]{:S(2)}, u32[]{:S(2)}) collective-permute-start(bf16[128,1024]{1,0:T(8,128)(2,1)S(1)} %get-tuple-element.21.refs_1_.refs_0_), channel_id=1, source_target_pairs={{0,4},{4,8},{8,12},{1,5},{5,9},{9,13},{2,6},{6,10},{10,14},{3,7},{... | collective-permute-start | bytes 786440 | tf_op jit(solution)/shard_map/ppermute | solution.py:323
  5.2 26.7 %collective-permute-start.5 = (bf16[128,1024]{1,0:T(8,128)(2,1)S(1)}, bf16[128,1024]{1,0:T(8,128)(2,1)S(1)}, u32[]{:S(2)}, u32[]{:S(2)}) collective-permute-start(bf16[128,1024]{1,0:T(8,128)(2,1)S(1)} %get-tuple-element.21.refs_1_.refs_0_), channel_id=1, source_target_pairs={{12,4},{13,5},{14,6},{15,7},{28,20},{29,21},{30,22},{31,23}} | collective-permute-start | bytes 786440 | tf_op jit(solution)/shard_map/ppermute | solution.py:323
  9.6 13.8 %collective-permute-start.6 = (bf16[64,1024]{1,0:T(8,128)(2,1)S(1)}, bf16[64,1024]{1,0:T(8,128)(2,1)S(1)}, u32[]{:S(2)}, u32[]{:S(2)}) collective-permute-start(bf16[64,1024]{1,0:T(8,128)(2,1)S(1)} %get-tuple-element.19.refs_0_), channel_id=1, source_target_pairs={{0,4},{4,8},{8,12},{1,5},{5,9},{9,13},{2,6},{6,10},{10,14},{3,7},{... | collective-permute-start | bytes 393224 | tf_op jit(solution)/shard_map/ppermute | solution.py:323
  10.9 19.4 %collective-permute-start.7 = (bf16[64,1024]{1,0:T(8,128)(2,1)S(1)}, bf16[64,1024]{1,0:T(8,128)(2,1)S(1)}, u32[]{:S(2)}, u32[]{:S(2)}) collective-permute-start(bf16[64,1024]{1,0:T(8,128)(2,1)S(1)} %get-tuple-element.19.refs_0_), channel_id=1, source_target_pairs={{12,4},{13,5},{14,6},{15,7},{28,20},{29,21},{30,22},{31,23}} | collective-permute-start | bytes 393224 | tf_op jit(solution)/shard_map/ppermute | solution.py:323
  13.8 5.5 %collective-permute-start = (s32[3,2,64]{2,1,0:T(2,128)S(1)}, s32[3,2,64]{2,1,0:T(2,128)S(1)}, u32[]{:S(2)}, u32[]{:S(2)}) collective-permute-start(s32[3,2,64]{2,1,0:T(2,128)S(1)} %get-tuple-element.18.vis_ref), channel_id=1, source_target_pairs={{0,4},{4,8},{8,12},{1,5},{5,9},{9,13},{2,6},{6,10},{10,14},{3,7},{... | collective-permute-start | bytes 4616 | tf_op jit(solution)/shard_map/ppermute | solution.py:324
  19.3 2.8 %collective-permute-start.1 = (s32[3,2,64]{2,1,0:T(2,128)S(1)}, s32[3,2,64]{2,1,0:T(2,128)S(1)}, u32[]{:S(2)}, u32[]{:S(2)}) collective-permute-start(s32[3,2,64]{2,1,0:T(2,128)S(1)} %get-tuple-element.18.vis_ref), channel_id=1, source_target_pairs={{12,4},{13,5},{14,6},{15,7},{28,20},{29,21},{30,22},{31,23}} | collective-permute-start | bytes 4616 | tf_op jit(solution)/shard_map/ppermute | solution.py:324
  20.8 8.3 %copy-start = (bf16[256,1024]{1,0:T(8,128)(2,1)S(1)}, bf16[256,1024]{1,0:T(8,128)(2,1)}, u32[]{:S(2)}) copy-start(bf16[256,1024]{1,0:T(8,128)(2,1)} %constant.7.clone.inv_ref.refs_0_) | copy-start | bytes 1572868
  22.1 12.0 %collective-permute-start.2 = (bf16[64,1024]{1,0:T(8,128)(2,1)S(1)}, bf16[64,1024]{1,0:T(8,128)(2,1)S(1)}, u32[]{:S(2)}, u32[]{:S(2)}) collective-permute-start(bf16[64,1024]{1,0:T(8,128)(2,1)S(1)} %shard_map.48.refs_2_.refs_3_), channel_id=1, source_target_pairs={{0,4},{4,8},{8,12},{1,5},{5,9},{9,13},{2,6},{6,10},{10,14},{3,7},{... | collective-permute-start | bytes 393224 | tf_op jit(solution)/shard_map/ppermute | solution.py:323
  23.4 10.7 %collective-permute-start.3 = (bf16[64,1024]{1,0:T(8,128)(2,1)S(1)}, bf16[64,1024]{1,0:T(8,128)(2,1)S(1)}, u32[]{:S(2)}, u32[]{:S(2)}) collective-permute-start(bf16[64,1024]{1,0:T(8,128)(2,1)S(1)} %shard_map.48.refs_2_.refs_3_), channel_id=1, source_target_pairs={{12,4},{13,5},{14,6},{15,7},{28,20},{29,21},{30,22},{31,23}} | collective-permute-start | bytes 393224 | tf_op jit(solution)/shard_map/ppermute | solution.py:323
  36.3 1.5 %collective-permute-start.8 = (bf16[128,640]{1,0:T(8,128)(2,1)S(1)}, bf16[128,640]{1,0:T(8,128)(2,1)S(1)}, u32[]{:S(2)}, u32[]{:S(2)}) collective-permute-start(bf16[128,640]{1,0:T(8,128)(2,1)S(1)} %bitcast.13), channel_id=1, source_target_pairs={{0,1},{1,0},{2,3},{3,2},{4,5},{5,4},{6,7},{7,6},{8,9},{9,8},{10,11... | collective-permute-start | bytes 491528 | tf_op jit(solution)/shard_map/ppermute | solution.py:371
  37.8 15.5 %collective-permute-start.10 = (bf16[64,256]{1,0:T(8,128)(2,1)S(1)}, bf16[64,256]{1,0:T(8,128)(2,1)S(1)}, u32[]{:S(2)}, u32[]{:S(2)}) collective-permute-start(bf16[64,256]{1,0:T(8,128)(2,1)S(1)} %get-tuple-element.35), channel_id=1, source_target_pairs={{4,2},{6,0},{8,6},{10,4},{12,10},{14,8},{5,3},{7,1},{9,7},{11,5},{... | collective-permute-start | bytes 98312 | tf_op jit(solution)/shard_map/ppermute | solution.py:397
  39.1 14.2 %collective-permute-start.9 = (bf16[64,256]{1,0:T(8,128)(2,1)S(1)}, bf16[64,256]{1,0:T(8,128)(2,1)S(1)}, u32[]{:S(2)}, u32[]{:S(2)}) collective-permute-start(bf16[64,256]{1,0:T(8,128)(2,1)S(1)} %get-tuple-element.34), channel_id=1, source_target_pairs={{4,0},{6,2},{8,4},{10,6},{12,8},{14,10},{5,1},{7,3},{9,5},{11,7},{... | collective-permute-start | bytes 98312 | tf_op jit(solution)/shard_map/ppermute | solution.py:397
  43.9 9.4 %collective-permute-start.13 = (bf16[64,256]{1,0:T(8,128)(2,1)S(1)}, bf16[64,256]{1,0:T(8,128)(2,1)S(1)}, u32[]{:S(2)}, u32[]{:S(2)}) collective-permute-start(bf16[64,256]{1,0:T(8,128)(2,1)S(1)} %bitcast.14), channel_id=1, source_target_pairs={{0,2},{2,0},{1,3},{3,1},{4,6},{6,4},{5,7},{7,5},{8,10},{10,8},{9,1... | collective-permute-start | bytes 98312 | tf_op jit(solution)/shard_map/ppermute | solution.py:400
  44.6 6.5 %collective-permute-start.11 = (bf16[64,128]{1,0:T(8,128)(2,1)S(1)}, bf16[64,128]{1,0:T(8,128)(2,1)S(1)}, u32[]{:S(2)}, u32[]{:S(2)}) collective-permute-start(bf16[64,128]{1,0:T(8,128)(2,1)S(1)} %get-tuple-element.36), channel_id=1, source_target_pairs={{4,12},{6,14},{5,13},{7,15},{20,28},{22,30},{21,29},{23,31}} | collective-permute-start | bytes 49160 | tf_op jit(solution)/shard_map/ppermute | solution.py:397
  45.8 7.5 %collective-permute-start.12 = (bf16[64,128]{1,0:T(8,128)(2,1)S(1)}, bf16[64,128]{1,0:T(8,128)(2,1)S(1)}, u32[]{:S(2)}, u32[]{:S(2)}) collective-permute-start(bf16[64,128]{1,0:T(8,128)(2,1)S(1)} %get-tuple-element.37), channel_id=1, source_target_pairs={{4,14},{6,12},{5,15},{7,13},{20,30},{22,28},{21,31},{23,29}} | collective-permute-start | bytes 49160 | tf_op jit(solution)/shard_map/ppermute | solution.py:397
where the time goes:
time: 54.8 us; the launch traced here: 54.4 us
  starting transfers between devices  29.1 us (53%)
  waiting for transfers between devices  12.4 us (23%)
  Pallas kernels  11.5 us (21%)
  other arithmetic  0.81 us (1%)
    ppermute x6, starting transfers between devices, local(): lax.ppermute(c, 'chan', to)  16.9 us
    pallas_call x9, Pallas kernels, call(): pl.pallas_call(kernel, out_shape=out_shape, in_specs=[pl.BlockSpec(memory...  11.5 us
    ppermute x4, starting transfers between devices, local(): add(groups[k + 1], lax.ppermute(away[k][dd], ('chan', 'day'), route))  8.68 us
    ppermute x4, waiting for transfers between devices, local(): add(groups[k + 1], lax.ppermute(away[k][dd], ('chan', 'day'), route))  6.16 us
    ppermute x2, waiting for transfers between devices, local(): asked.append([lax.ppermute(visits, 'chan', to) for to in arrivals])  4.88 us
    ppermute x2, starting transfers between devices, local(): asked.append([lax.ppermute(visits, 'chan', to) for to in arrivals])  2.82 us
    ppermute x1, waiting for transfers between devices, local(): got.append(lax.ppermute(send[ds - 1], 'seg', route))  1.38 us
  transfers between devices with their start and end apart: 14, of which 5 were waited for; matrix products, arithmetic and copies ran while one was open for 0% of the time, Pallas kernels for 10%

commit v1 on v0

--- a/solution.py
+++ b/solution.py
@@ -185,10 +185,10 @@
     return jnp.concatenate([real, imag], 1).astype(BF16)
 
 
-def lag_terms(inv_ref, receivers, sources, select):
+def lag_terms(inv_ref, jobs):
     total = None
     for r in range(FOLD):
-        block = cross_block(receivers, sources, select, r)
+        block = jnp.concatenate([cross_block(*job, r) for job in jobs], 0)
         part = lax.dot_general(
             inv_ref[:, r * PAIR : (r + 1) * PAIR],
             block,
@@ -209,8 +209,8 @@
     reach = vis_ref.shape[0] // 2
     units = [u for ref in chunks for u in units_of(ref, chans)]
     for n in range(reach):
-        select_ref[n] = one_hot(vis_ref[reach + 1 + n], chans)
-    out_ref[...] = lag_terms(inv_ref, units, units, one_hot(vis_ref[reach], chans))
+        select_ref[n] = one_hot(vis_ref[reach - 1 - n], chans)
+    out_ref[...] = lag_terms(inv_ref, [(units, units, one_hot(vis_ref[reach], chans))])
 
 
 def select_kernel(wanted, *refs):
@@ -219,23 +219,18 @@
         out_ref[n] = one_hot(refs[which][visit], refs[which].shape[2])
 
 
-def pair_terms(jobs, inv_ref, selects, blocks):
-    chans = selects[0].shape[2]
-    units = [units_of(ref, chans) for ref in blocks]
-    return [
-        lag_terms(inv_ref, units[receiver], units[source], selects[which][index])
-        for receiver, source, which, index in jobs
-    ]
-
-
 def pair_kernel(jobs, n_blocks, inv_ref, near_ref, far_ref, *refs):
     blocks, out_ref = refs[:n_blocks], refs[-1]
-    wide = near_ref.shape[1]
-    for n, value in enumerate(pair_terms(jobs, inv_ref, (near_ref, far_ref), blocks)):
-        cols = slice(n * wide, (n + 1) * wide)
-        if len(refs) > n_blocks + 1:
-            value = value + refs[n_blocks][:, cols]
-        out_ref[:, cols] = value
+    chans = near_ref.shape[2]
+    units = [units_of(ref, chans) for ref in blocks]
+    selects = (near_ref, far_ref)
+    value = lag_terms(
+        inv_ref,
+        [(units[to], units[source], selects[k][n]) for to, source, k, n in jobs],
+    )
+    if len(refs) > n_blocks + 1:
+        value = value + refs[n_blocks][...]
+    out_ref[...] = value
 
 
 def split_kernel(share, n_day, n_seg, n_parts, *refs):
@@ -282,25 +277,13 @@
                     outs[g + 1][dd, :, to] = value.astype(BF16)
 
 
-def line_plan(n_chan):
-    up = [(i, i + 1) for i in range(n_chan - 1)]
-    back = [(i + 1, i) for i in range(n_chan - 1)]
-    arrivals = [up, [(n_chan - 1, 1)]]
-    wanted = [(0, 0), (0, 2), (1, 0)]
-    jobs = [(0, 1, 0, 0), (1, 0, 1, 0), (1, 2, 1, 1), (2, 1, 1, 2)]
-    visits_of = [2, 0, 2, 0]
-    ways = [None, 0, 0, 1]
-    routes = [back, [(1, n_chan - 1)]]
-    return [(arrivals, wanted, jobs, visits_of, ways)], routes
-
-
 def ring_plan(n_chan, reach):
     groups, routes = [], []
     for o in range(1, reach + 1):
-        to = [(i, (i + o) % n_chan) for i in range(n_chan)]
+        to = [((i + o) % n_chan, i) for i in range(n_chan)]
         routes.append([(j, i) for i, j in to])
         jobs = [(0, 1, 0, o - 1), (1, 0, 1, 0)]
-        groups.append(([to], [(0, reach - o)], jobs, [reach + o, reach - o], [None, o - 1]))
+        groups.append(([to], [(0, reach + o)], jobs, [reach - o, reach + o], [None, o - 1]))
     return groups, routes
 
 
@@ -314,8 +297,7 @@
     table = trig_columns(np.arange(SPAN)).reshape(SPAN, FOLD, PAIR).transpose(1, 0, 2)
     table = jnp.asarray(np.ascontiguousarray(table))
     inverse = jnp.asarray(trig_columns(np.arange(LAGS) - LAGS // 2))
-    line = reach == 1 and n_chan > 2
-    plan, routes = line_plan(n_chan) if line else ring_plan(n_chan, reach)
+    plan, routes = ring_plan(n_chan, reach)
 
     chunks, visits = spectra_chunks(records, table, visits)
     held, asked = [], []

time: 54.8 us -> 32.6 us (0.59)
  the two profiles are of different devices: /device:TPU:24 before, /device:TPU:0 now
where the time goes in v1:
time: 32.6 us; the launch traced here: 32.4 us
  waiting for transfers between devices  13.4 us (41%)
  starting transfers between devices  9.77 us (30%)
  Pallas kernels  7.96 us (24%)
  other arithmetic  0.8 us (2%)
    ppermute x1, waiting for transfers between devices, local(): asked.append([lax.ppermute(visits, 'chan', to) for to in arrivals])  8.62 us
    pallas_call x9, Pallas kernels, call(): pl.pallas_call(kernel, out_shape=out_shape, in_specs=[pl.BlockSpec(memory...  7.96 us
    ppermute x3, starting transfers between devices, local(): lax.ppermute(c, 'chan', to)  6.08 us
    ppermute x2, waiting for transfers between devices, local(): add(groups[k + 1], lax.ppermute(away[k][dd], ('chan', 'day'), route))  3.53 us
    ppermute x2, starting transfers between devices, local(): add(groups[k + 1], lax.ppermute(away[k][dd], ('chan', 'day'), route))  3.01 us
    ppermute x1, waiting for transfers between devices, local(): got.append(lax.ppermute(send[ds - 1], 'seg', route))  1.29 us
    convert_element_type x1, other arithmetic, local(): result = (jnp.concatenate(columns, 1) * scale).astype(BF16)  0.78 us
  transfers between devices with their start and end apart: 8, of which 3 were waited for; matrix products, arithmetic and copies ran while one was open for 0% of the time, Pallas kernels for 10%

profile of v1, /device:TPU:0, one launch (start us, length us, event | category | flops | bytes accessed | tf_op | source)
XLA Modules:
  0.0 32.4 jit_solution(11011069499501820978)
XLA Ops:
  0.0 1.9 %shard_map.46 = (bf16[64,1024]{1,0:T(8,128)(2,1)S(1)}, bf16[4,512,256]{2,1,0:T(8,128)(2,1)S(1)}, s32[3,2,64]{2,1,0:T(2,128)S(1)}) custom-call(bf16[2,2,64,2048]{3,2,1,0:T(8,128)(2,1)} %x_hbm.3, bf16[4,512,256]{2,1,0:T(8,128)(2,1)} %constant.6.clone.t_hbm, s32[3,2,64]{2,1,0:T(2,128)} %vis_hbm.1), custom_call_target="tpu_custom_call" | custom-call | flops 268435456 | bytes 2098688 | tf_op jit(solution)/shard_map/pallas_call | solution.py:48
  1.9 1.9 %shard_map.47 = (bf16[128,1024]{1,0:T(8,128)(2,1)S(1)}, bf16[1,64,2048]{2,1,0:T(8,128)(2,1)S(1)}) custom-call(bf16[2,2,64,2048]{3,2,1,0:T(8,128)(2,1)} %x_hbm.3, bf16[4,512,256]{2,1,0:T(8,128)(2,1)S(1)} %get-tuple-element.19.t_ref), custom_call_target="tpu_custom_call" | custom-call | flops 536870912 | bytes 2097152 | tf_op jit(solution)/shard_map/pallas_call | solution.py:48
  3.9 5.1 %collective-permute-start.2 = (bf16[128,1024]{1,0:T(8,128)(2,1)S(1)}, bf16[128,1024]{1,0:T(8,128)(2,1)S(1)}, u32[]{:S(2)}, u32[]{:S(2)}) collective-permute-start(bf16[128,1024]{1,0:T(8,128)(2,1)S(1)} %get-tuple-element.20.refs_1_.refs_0_), channel_id=1, source_target_pairs={{4,0},{8,4},{12,8},{0,12},{5,1},{9,5},{13,9},{1,13},{6,2},{10,6},{... | collective-permute-start | bytes 786440 | tf_op jit(solution)/shard_map/ppermute | solution.py:305
  9.0 0.4 %collective-permute-start.3 = (bf16[64,1024]{1,0:T(8,128)(2,1)S(1)}, bf16[64,1024]{1,0:T(8,128)(2,1)S(1)}, u32[]{:S(2)}, u32[]{:S(2)}) collective-permute-start(bf16[64,1024]{1,0:T(8,128)(2,1)S(1)} %get-tuple-element.18.refs_0_), channel_id=1, source_target_pairs={{4,0},{8,4},{12,8},{0,12},{5,1},{9,5},{13,9},{1,13},{6,2},{10,6},{... | collective-permute-start | bytes 393224 | tf_op jit(solution)/shard_map/ppermute | solution.py:305
  9.5 0.0 copy-start
  9.5 0.6 %shard_map.48.refs_2_.refs_3_ = bf16[64,1024]{1,0:T(8,128)(2,1)S(1)} custom-call(bf16[1,64,2048]{2,1,0:T(8,128)(2,1)S(1)} %get-tuple-element.21.x_ref, bf16[4,512,256]{2,1,0:T(8,128)(2,1)S(1)} %get-tuple-element.19.t_ref), custom_call_target="tpu_custom_call" | custom-call | flops 268435456 | bytes 1310720 | tf_op jit(solution)/shard_map/pallas_call | solution.py:48
  10.1 0.5 %collective-permute-start.1 = (bf16[64,1024]{1,0:T(8,128)(2,1)S(1)}, bf16[64,1024]{1,0:T(8,128)(2,1)S(1)}, u32[]{:S(2)}, u32[]{:S(2)}) collective-permute-start(bf16[64,1024]{1,0:T(8,128)(2,1)S(1)} %shard_map.48.refs_2_.refs_3_), channel_id=1, source_target_pairs={{4,0},{8,4},{12,8},{0,12},{5,1},{9,5},{13,9},{1,13},{6,2},{10,6},{... | collective-permute-start | bytes 393224 | tf_op jit(solution)/shard_map/ppermute | solution.py:305
  10.6 0.1 collective-permute-start
  10.6 0.0 copy-done
  10.6 1.0 %shard_map.49 = (f32[256,128]{1,0:T(8,128)S(1)}, bf16[1,128,64]{2,1,0:T(8,128)(2,1)S(1)}) custom-call(bf16[256,1024]{1,0:T(8,128)(2,1)S(1)} %copy-done, s32[3,2,64]{2,1,0:T(2,128)S(1)} %get-tuple-element.17.vis_ref, bf16[64,1024]{1,0:T(8,128)(2,1)S(1)} %get-tuple-element.18.refs_0_, bf16[128,1024]{1,0:T(8,128)(2,1)S(1)} %get-tuple-element.20.refs_1_.refs_0_, ...), custom_call_target="tpu_custom_call" | custom-call | flops 67108864 | bytes 1050112 | tf_op jit(solution)/shard_map/pallas_call | solution.py:48
  11.6 8.6 %collective-permute-done.refs_0_ = s32[3,2,64]{2,1,0:T(2,128)S(1)} collective-permute-done((s32[3,2,64]{2,1,0:T(2,128)S(1)}, s32[3,2,64]{2,1,0:T(2,128)S(1)}, u32[]{:S(2)}, u32[]{:S(2)}) %collective-permute-start) | collective-permute-done | bytes 1568 | tf_op jit(solution)/shard_map/ppermute | solution.py:306
  20.3 0.2 shard_map.50.far_ref.refs_2_
  20.4 0.0 collective-permute-done.3.refs_1_
  20.5 0.8 %shard_map.51.refs_2_ = f32[256,256]{1,0:T(8,128)S(1)} custom-call(bf16[256,1024]{1,0:T(8,128)(2,1)S(1)} %copy-done, bf16[1,128,64]{2,1,0:T(8,128)(2,1)S(1)} %get-tuple-element.22.near_ref.refs_1_, bf16[1,128,64]{2,1,0:T(8,128)(2,1)S(1)} %shard_map.50.far_ref.refs_2_, bf16[64,1024]{1,0:T(8,128)(2,1)S(1)} %get-tuple-element.18.refs_0_, ...), custom_call_target="tpu_custom_call" | custom-call | flops 134217728 | bytes 819200 | tf_op jit(solution)/shard_map/pallas_call | solution.py:48
  21.2 0.0 collective-permute-done.2.refs_1_
  21.2 0.8 %shard_map.52.refs_5_ = f32[256,256]{1,0:T(8,128)S(1)} custom-call(bf16[256,1024]{1,0:T(8,128)(2,1)S(1)} %copy-done, bf16[1,128,64]{2,1,0:T(8,128)(2,1)S(1)} %get-tuple-element.22.near_ref.refs_1_, bf16[1,128,64]{2,1,0:T(8,128)(2,1)S(1)} %shard_map.50.far_ref.refs_2_, bf16[128,1024]{1,0:T(8,128)(2,1)S(1)} %get-tuple-element.20.refs_1_.refs_0_, ...), custom_call_target="tpu_custom_call" | custom-call | flops 134217728 | bytes 1343488 | tf_op jit(solution)/shard_map/pallas_call | solution.py:48
  22.0 0.0 collective-permute-done.1.refs_4_
  22.0 0.8 %shard_map.53 = (f32[128,384]{1,0:T(8,128)S(1)}, bf16[1,128,384]{2,1,0:T(8,128)(2,1)S(1)}) custom-call(bf16[256,1024]{1,0:T(8,128)(2,1)S(1)} %copy-done, bf16[1,128,64]{2,1,0:T(8,128)(2,1)S(1)} %get-tuple-element.22.near_ref.refs_1_, bf16[1,128,64]{2,1,0:T(8,128)(2,1)S(1)} %shard_map.50.far_ref.refs_2_, bf16[64,1024]{1,0:T(8,128)(2,1)S(1)} %shard_map.48.refs_2_.refs_3_, ...), custom_call_target="tpu_custom_call" | custom-call | flops 134217728 | bytes 1212416 | tf_op jit(solution)/shard_map/pallas_call | solution.py:48
  22.8 0.1 collective-permute-start.4
  22.9 1.3 %collective-permute-done.4.refs_1_ = bf16[128,384]{1,0:T(8,128)(2,1)S(1)} collective-permute-done((bf16[128,384]{1,0:T(8,128)(2,1)S(1)}, bf16[128,384]{1,0:T(8,128)(2,1)S(1)}, u32[]{:S(2)}, u32[]{:S(2)}) %collective-permute-start.4) | collective-permute-done | bytes 98336 | tf_op jit(solution)/shard_map/ppermute | solution.py:353
  24.2 1.4 %collective-permute-start.7 = (bf16[64,128]{1,0:T(8,128)(2,1)S(1)}, bf16[64,128]{1,0:T(8,128)(2,1)S(1)}, u32[]{:S(2)}, u32[]{:S(2)}) collective-permute-start(bf16[64,128]{1,0:T(8,128)(2,1)S(1)} %get-tuple-element.32), channel_id=1, source_target_pairs={{0,6},{2,4},{4,10},{6,8},{8,14},{10,12},{12,2},{14,0},{1,7},{3,5},... | collective-permute-start | bytes 49160 | tf_op jit(solution)/shard_map/ppermute | solution.py:379
  25.6 1.6 %collective-permute-start.6 = (bf16[64,128]{1,0:T(8,128)(2,1)S(1)}, bf16[64,128]{1,0:T(8,128)(2,1)S(1)}, u32[]{:S(2)}, u32[]{:S(2)}) collective-permute-start(bf16[64,128]{1,0:T(8,128)(2,1)S(1)} %get-tuple-element.31), channel_id=1, source_target_pairs={{0,4},{2,6},{4,8},{6,10},{8,12},{10,14},{12,0},{14,2},{1,5},{3,7},... | collective-permute-start | bytes 49160 | tf_op jit(solution)/shard_map/ppermute | solution.py:379
  27.2 0.5 %collective-permute-start.5 = (bf16[64,256]{1,0:T(8,128)(2,1)S(1)}, bf16[64,256]{1,0:T(8,128)(2,1)S(1)}, u32[]{:S(2)}, u32[]{:S(2)}) collective-permute-start(bf16[64,256]{1,0:T(8,128)(2,1)S(1)} %bitcast.10), channel_id=1, source_target_pairs={{0,2},{2,0},{1,3},{3,1},{4,6},{6,4},{5,7},{7,5},{8,10},{10,8},{9,1... | collective-permute-start | bytes 98312 | tf_op jit(solution)/shard_map/ppermute | solution.py:382
  27.8 3.5 %collective-permute-done.7 = bf16[64,128]{1,0:T(8,128)(2,1)S(1)} collective-permute-done((bf16[64,128]{1,0:T(8,128)(2,1)S(1)}, bf16[64,128]{1,0:T(8,128)(2,1)S(1)}, u32[]{:S(2)}, u32[]{:S(2)}) %collective-permute-start.7) | collective-permute-done | bytes 16416 | tf_op jit(solution)/shard_map/ppermute | solution.py:379
  31.3 0.0 collective-permute-done.6
  31.3 0.1 concatenate.12
  31.4 0.0 collective-permute-done.5
  31.4 0.1 concatenate.11
  31.5 0.1 concatenate.10
  31.6 0.8 %fusion = bf16[64,3,2,64]{3,2,1,0:T(2,128)(2,1)} fusion(f32[64,1,2,64]{3,2,1,0:T(2,128)S(1)} %bitcast.11, f32[64,1,2,64]{3,2,1,0:T(2,128)S(1)} %bitcast.12, f32[64,1,2,64]{3,2,1,0:T(2,128)S(1)} %bitcast.13), kind=kLoop, calls=%fused_computation.1 | loop fusion | flops 98304 | bytes 147456 | tf_op jit(solution)/shard_map/convert_element_type | solution.py:386
  (4 shorter events, 0.0 us)
Async XLA Ops:
  3.9 17.3 %collective-permute-start.2 = (bf16[128,1024]{1,0:T(8,128)(2,1)S(1)}, bf16[128,1024]{1,0:T(8,128)(2,1)S(1)}, u32[]{:S(2)}, u32[]{:S(2)}) collective-permute-start(bf16[128,1024]{1,0:T(8,128)(2,1)S(1)} %get-tuple-element.20.refs_1_.refs_0_), channel_id=1, source_target_pairs={{4,0},{8,4},{12,8},{0,12},{5,1},{9,5},{13,9},{1,13},{6,2},{10,6},{... | collective-permute-start | bytes 786440 | tf_op jit(solution)/shard_map/ppermute | solution.py:305
  9.0 11.4 %collective-permute-start.3 = (bf16[64,1024]{1,0:T(8,128)(2,1)S(1)}, bf16[64,1024]{1,0:T(8,128)(2,1)S(1)}, u32[]{:S(2)}, u32[]{:S(2)}) collective-permute-start(bf16[64,1024]{1,0:T(8,128)(2,1)S(1)} %get-tuple-element.18.refs_0_), channel_id=1, source_target_pairs={{4,0},{8,4},{12,8},{0,12},{5,1},{9,5},{13,9},{1,13},{6,2},{10,6},{... | collective-permute-start | bytes 393224 | tf_op jit(solution)/shard_map/ppermute | solution.py:305
  9.5 1.2 %copy-start = (bf16[256,1024]{1,0:T(8,128)(2,1)S(1)}, bf16[256,1024]{1,0:T(8,128)(2,1)}, u32[]{:S(2)}) copy-start(bf16[256,1024]{1,0:T(8,128)(2,1)} %constant.7.clone.inv_ref.refs_0_) | copy-start | bytes 1572868
  10.1 11.9 %collective-permute-start.1 = (bf16[64,1024]{1,0:T(8,128)(2,1)S(1)}, bf16[64,1024]{1,0:T(8,128)(2,1)S(1)}, u32[]{:S(2)}, u32[]{:S(2)}) collective-permute-start(bf16[64,1024]{1,0:T(8,128)(2,1)S(1)} %shard_map.48.refs_2_.refs_3_), channel_id=1, source_target_pairs={{4,0},{8,4},{12,8},{0,12},{5,1},{9,5},{13,9},{1,13},{6,2},{10,6},{... | collective-permute-start | bytes 393224 | tf_op jit(solution)/shard_map/ppermute | solution.py:305
  10.6 9.7 %collective-permute-start = (s32[3,2,64]{2,1,0:T(2,128)S(1)}, s32[3,2,64]{2,1,0:T(2,128)S(1)}, u32[]{:S(2)}, u32[]{:S(2)}) collective-permute-start(s32[3,2,64]{2,1,0:T(2,128)S(1)} %get-tuple-element.17.vis_ref), channel_id=1, source_target_pairs={{4,0},{8,4},{12,8},{0,12},{5,1},{9,5},{13,9},{1,13},{6,2},{10,6},{... | collective-permute-start | bytes 4616 | tf_op jit(solution)/shard_map/ppermute | solution.py:306
  22.8 1.4 %collective-permute-start.4 = (bf16[128,384]{1,0:T(8,128)(2,1)S(1)}, bf16[128,384]{1,0:T(8,128)(2,1)S(1)}, u32[]{:S(2)}, u32[]{:S(2)}) collective-permute-start(bf16[128,384]{1,0:T(8,128)(2,1)S(1)} %bitcast.9), channel_id=1, source_target_pairs={{0,1},{1,0},{2,3},{3,2},{4,5},{5,4},{6,7},{7,6},{8,9},{9,8},{10,11... | collective-permute-start | bytes 294920 | tf_op jit(solution)/shard_map/ppermute | solution.py:353
  24.2 7.1 %collective-permute-start.7 = (bf16[64,128]{1,0:T(8,128)(2,1)S(1)}, bf16[64,128]{1,0:T(8,128)(2,1)S(1)}, u32[]{:S(2)}, u32[]{:S(2)}) collective-permute-start(bf16[64,128]{1,0:T(8,128)(2,1)S(1)} %get-tuple-element.32), channel_id=1, source_target_pairs={{0,6},{2,4},{4,10},{6,8},{8,14},{10,12},{12,2},{14,0},{1,7},{3,5},... | collective-permute-start | bytes 49160 | tf_op jit(solution)/shard_map/ppermute | solution.py:379
  25.6 5.6 %collective-permute-start.6 = (bf16[64,128]{1,0:T(8,128)(2,1)S(1)}, bf16[64,128]{1,0:T(8,128)(2,1)S(1)}, u32[]{:S(2)}, u32[]{:S(2)}) collective-permute-start(bf16[64,128]{1,0:T(8,128)(2,1)S(1)} %get-tuple-element.31), channel_id=1, source_target_pairs={{0,4},{2,6},{4,8},{6,10},{8,12},{10,14},{12,0},{14,2},{1,5},{3,7},... | collective-permute-start | bytes 49160 | tf_op jit(solution)/shard_map/ppermute | solution.py:379
  27.2 4.2 %collective-permute-start.5 = (bf16[64,256]{1,0:T(8,128)(2,1)S(1)}, bf16[64,256]{1,0:T(8,128)(2,1)S(1)}, u32[]{:S(2)}, u32[]{:S(2)}) collective-permute-start(bf16[64,256]{1,0:T(8,128)(2,1)S(1)} %bitcast.10), channel_id=1, source_target_pairs={{0,2},{2,0},{1,3},{3,1},{4,6},{6,4},{5,7},{7,5},{8,10},{10,8},{9,1... | collective-permute-start | bytes 98312 | tf_op jit(solution)/shard_map/ppermute | solution.py:382

commit v2 on v1

--- a/solution.py
+++ b/solution.py
@@ -209,7 +209,7 @@
     reach = vis_ref.shape[0] // 2
     units = [u for ref in chunks for u in units_of(ref, chans)]
     for n in range(reach):
-        select_ref[n] = one_hot(vis_ref[reach - 1 - n], chans)
+        select_ref[n] = one_hot(vis_ref[reach + 1 + n], chans)
     out_ref[...] = lag_terms(inv_ref, [(units, units, one_hot(vis_ref[reach], chans))])
 
 
@@ -280,10 +280,10 @@
 def ring_plan(n_chan, reach):
     groups, routes = [], []
     for o in range(1, reach + 1):
-        to = [((i + o) % n_chan, i) for i in range(n_chan)]
+        to = [(i, (i + o) % n_chan) for i in range(n_chan)]
         routes.append([(j, i) for i, j in to])
         jobs = [(0, 1, 0, o - 1), (1, 0, 1, 0)]
-        groups.append(([to], [(0, reach + o)], jobs, [reach - o, reach + o], [None, o - 1]))
+        groups.append(([to], [(0, reach - o)], jobs, [reach + o, reach - o], [None, o - 1]))
     return groups, routes
 
 

time: 32.6 us -> 33.2 us (1.018)
  starting transfers between devices: 9.77 us -> 10.2 us
    ppermute x2, waiting for transfers between devices: 3.53 us -> 2.75 us  [local(): add(groups[k + 1], lax.ppermute(away[k][dd], ('chan', 'day'), route))]
    ppermute x1, waiting for transfers between devices: 0.01 us -> 0.51 us  [local(): add(groups[0], lax.ppermute(by_day[dd - 1], 'day', route))]
    ppermute x1, waiting for transfers between devices: 8.62 us -> 9.12 us  [local(): asked.append([lax.ppermute(visits, 'chan', to) for to in arrivals])]
  transfers between devices with their start and end apart: 8 -> 8, of which waited for: 3 -> 5; matrix products, arithmetic and copies ran while one was open for 0% -> 0% of each run, Pallas kernels for 10% -> 10%
where the time goes in v2:
time: 33.2 us; the launch traced here: 33 us
  waiting for transfers between devices  13.7 us (41%)
  starting transfers between devices  10.2 us (31%)
  Pallas kernels  7.97 us (24%)
  other arithmetic  0.8 us (2%)
    ppermute x1, waiting for transfers between devices, local(): asked.append([lax.ppermute(visits, 'chan', to) for to in arrivals])  9.12 us
    pallas_call x9, Pallas kernels, call(): pl.pallas_call(kernel, out_shape=out_shape, in_specs=[pl.BlockSpec(memory...  7.97 us
    ppermute x3, starting transfers between devices, local(): lax.ppermute(c, 'chan', to)  6.31 us
    ppermute x2, starting transfers between devices, local(): add(groups[k + 1], lax.ppermute(away[k][dd], ('chan', 'day'), route))  3.17 us
    ppermute x2, waiting for transfers between devices, local(): add(groups[k + 1], lax.ppermute(away[k][dd], ('chan', 'day'), route))  2.75 us
    ppermute x1, waiting for transfers between devices, local(): got.append(lax.ppermute(send[ds - 1], 'seg', route))  1.29 us
    convert_element_type x1, other arithmetic, local(): result = (jnp.concatenate(columns, 1) * scale).astype(BF16)  0.78 us
  transfers between devices with their start and end apart: 8, of which 5 were waited for; matrix products, arithmetic and copies ran while one was open for 0% of the time, Pallas kernels for 10%

profile of v2, /device:TPU:0, one launch (start us, length us, event | category | flops | bytes accessed | tf_op | source)
XLA Modules:
  0.0 33.0 jit_solution(15261970302845384338)
XLA Ops:
  0.0 1.9 %shard_map.46 = (bf16[64,1024]{1,0:T(8,128)(2,1)S(1)}, bf16[4,512,256]{2,1,0:T(8,128)(2,1)S(1)}, s32[3,2,64]{2,1,0:T(2,128)S(1)}) custom-call(bf16[2,2,64,2048]{3,2,1,0:T(8,128)(2,1)} %x_hbm.3, bf16[4,512,256]{2,1,0:T(8,128)(2,1)} %constant.6.clone.t_hbm, s32[3,2,64]{2,1,0:T(2,128)} %vis_hbm.1), custom_call_target="tpu_custom_call" | custom-call | flops 268435456 | bytes 2098688 | tf_op jit(solution)/shard_map/pallas_call | solution.py:48
  1.9 1.9 %shard_map.47 = (bf16[128,1024]{1,0:T(8,128)(2,1)S(1)}, bf16[1,64,2048]{2,1,0:T(8,128)(2,1)S(1)}) custom-call(bf16[2,2,64,2048]{3,2,1,0:T(8,128)(2,1)} %x_hbm.3, bf16[4,512,256]{2,1,0:T(8,128)(2,1)S(1)} %get-tuple-element.19.t_ref), custom_call_target="tpu_custom_call" | custom-call | flops 536870912 | bytes 2097152 | tf_op jit(solution)/shard_map/pallas_call | solution.py:48
  3.9 3.1 %collective-permute-start.2 = (bf16[128,1024]{1,0:T(8,128)(2,1)S(1)}, bf16[128,1024]{1,0:T(8,128)(2,1)S(1)}, u32[]{:S(2)}, u32[]{:S(2)}) collective-permute-start(bf16[128,1024]{1,0:T(8,128)(2,1)S(1)} %get-tuple-element.20.refs_1_.refs_0_), channel_id=1, source_target_pairs={{0,4},{4,8},{8,12},{12,0},{1,5},{5,9},{9,13},{13,1},{2,6},{6,10},{... | collective-permute-start | bytes 786440 | tf_op jit(solution)/shard_map/ppermute | solution.py:305
  7.0 1.6 %collective-permute-start.3 = (bf16[64,1024]{1,0:T(8,128)(2,1)S(1)}, bf16[64,1024]{1,0:T(8,128)(2,1)S(1)}, u32[]{:S(2)}, u32[]{:S(2)}) collective-permute-start(bf16[64,1024]{1,0:T(8,128)(2,1)S(1)} %get-tuple-element.18.refs_0_), channel_id=1, source_target_pairs={{0,4},{4,8},{8,12},{12,0},{1,5},{5,9},{9,13},{13,1},{2,6},{6,10},{... | collective-permute-start | bytes 393224 | tf_op jit(solution)/shard_map/ppermute | solution.py:305
  8.6 0.0 copy-start
  8.6 0.6 %shard_map.48.refs_2_.refs_3_ = bf16[64,1024]{1,0:T(8,128)(2,1)S(1)} custom-call(bf16[1,64,2048]{2,1,0:T(8,128)(2,1)S(1)} %get-tuple-element.21.x_ref, bf16[4,512,256]{2,1,0:T(8,128)(2,1)S(1)} %get-tuple-element.19.t_ref), custom_call_target="tpu_custom_call" | custom-call | flops 268435456 | bytes 1310720 | tf_op jit(solution)/shard_map/pallas_call | solution.py:48
  9.2 1.6 %collective-permute-start.1 = (bf16[64,1024]{1,0:T(8,128)(2,1)S(1)}, bf16[64,1024]{1,0:T(8,128)(2,1)S(1)}, u32[]{:S(2)}, u32[]{:S(2)}) collective-permute-start(bf16[64,1024]{1,0:T(8,128)(2,1)S(1)} %shard_map.48.refs_2_.refs_3_), channel_id=1, source_target_pairs={{0,4},{4,8},{8,12},{12,0},{1,5},{5,9},{9,13},{13,1},{2,6},{6,10},{... | collective-permute-start | bytes 393224 | tf_op jit(solution)/shard_map/ppermute | solution.py:305
  10.8 0.1 collective-permute-start
  10.9 0.0 copy-done
  10.9 1.0 %shard_map.49 = (f32[256,128]{1,0:T(8,128)S(1)}, bf16[1,128,64]{2,1,0:T(8,128)(2,1)S(1)}) custom-call(bf16[256,1024]{1,0:T(8,128)(2,1)S(1)} %copy-done, s32[3,2,64]{2,1,0:T(2,128)S(1)} %get-tuple-element.17.vis_ref, bf16[64,1024]{1,0:T(8,128)(2,1)S(1)} %get-tuple-element.18.refs_0_, bf16[128,1024]{1,0:T(8,128)(2,1)S(1)} %get-tuple-element.20.refs_1_.refs_0_, ...), custom_call_target="tpu_custom_call" | custom-call | flops 67108864 | bytes 1050112 | tf_op jit(solution)/shard_map/pallas_call | solution.py:48
  11.9 9.1 %collective-permute-done.refs_0_ = s32[3,2,64]{2,1,0:T(2,128)S(1)} collective-permute-done((s32[3,2,64]{2,1,0:T(2,128)S(1)}, s32[3,2,64]{2,1,0:T(2,128)S(1)}, u32[]{:S(2)}, u32[]{:S(2)}) %collective-permute-start) | collective-permute-done | bytes 1568 | tf_op jit(solution)/shard_map/ppermute | solution.py:306
  21.0 0.2 shard_map.50.far_ref.refs_2_
  21.2 0.0 collective-permute-done.3.refs_1_
  21.2 0.8 %shard_map.51.refs_2_ = f32[256,256]{1,0:T(8,128)S(1)} custom-call(bf16[256,1024]{1,0:T(8,128)(2,1)S(1)} %copy-done, bf16[1,128,64]{2,1,0:T(8,128)(2,1)S(1)} %get-tuple-element.22.near_ref.refs_1_, bf16[1,128,64]{2,1,0:T(8,128)(2,1)S(1)} %shard_map.50.far_ref.refs_2_, bf16[64,1024]{1,0:T(8,128)(2,1)S(1)} %get-tuple-element.18.refs_0_, ...), custom_call_target="tpu_custom_call" | custom-call | flops 134217728 | bytes 819200 | tf_op jit(solution)/shard_map/pallas_call | solution.py:48
  22.0 0.0 collective-permute-done.2.refs_1_
  22.0 0.8 %shard_map.52.refs_5_ = f32[256,256]{1,0:T(8,128)S(1)} custom-call(bf16[256,1024]{1,0:T(8,128)(2,1)S(1)} %copy-done, bf16[1,128,64]{2,1,0:T(8,128)(2,1)S(1)} %get-tuple-element.22.near_ref.refs_1_, bf16[1,128,64]{2,1,0:T(8,128)(2,1)S(1)} %shard_map.50.far_ref.refs_2_, bf16[128,1024]{1,0:T(8,128)(2,1)S(1)} %get-tuple-element.20.refs_1_.refs_0_, ...), custom_call_target="tpu_custom_call" | custom-call | flops 134217728 | bytes 1343488 | tf_op jit(solution)/shard_map/pallas_call | solution.py:48
  22.7 0.0 collective-permute-done.1.refs_4_
  22.8 0.8 %shard_map.53 = (f32[128,384]{1,0:T(8,128)S(1)}, bf16[1,128,384]{2,1,0:T(8,128)(2,1)S(1)}) custom-call(bf16[256,1024]{1,0:T(8,128)(2,1)S(1)} %copy-done, bf16[1,128,64]{2,1,0:T(8,128)(2,1)S(1)} %get-tuple-element.22.near_ref.refs_1_, bf16[1,128,64]{2,1,0:T(8,128)(2,1)S(1)} %shard_map.50.far_ref.refs_2_, bf16[64,1024]{1,0:T(8,128)(2,1)S(1)} %shard_map.48.refs_2_.refs_3_, ...), custom_call_target="tpu_custom_call" | custom-call | flops 134217728 | bytes 1212416 | tf_op jit(solution)/shard_map/pallas_call | solution.py:48
  23.5 0.1 collective-permute-start.4
  23.6 1.3 %collective-permute-done.4.refs_1_ = bf16[128,384]{1,0:T(8,128)(2,1)S(1)} collective-permute-done((bf16[128,384]{1,0:T(8,128)(2,1)S(1)}, bf16[128,384]{1,0:T(8,128)(2,1)S(1)}, u32[]{:S(2)}, u32[]{:S(2)}) %collective-permute-start.4) | collective-permute-done | bytes 98336 | tf_op jit(solution)/shard_map/ppermute | solution.py:353
  25.0 2.7 %collective-permute-start.6 = (bf16[64,128]{1,0:T(8,128)(2,1)S(1)}, bf16[64,128]{1,0:T(8,128)(2,1)S(1)}, u32[]{:S(2)}, u32[]{:S(2)}) collective-permute-start(bf16[64,128]{1,0:T(8,128)(2,1)S(1)} %get-tuple-element.32), channel_id=1, source_target_pairs={{4,2},{6,0},{8,6},{10,4},{12,10},{14,8},{0,14},{2,12},{5,3},{7,1},... | collective-permute-start | bytes 49160 | tf_op jit(solution)/shard_map/ppermute | solution.py:379
  27.7 0.4 %collective-permute-start.5 = (bf16[64,128]{1,0:T(8,128)(2,1)S(1)}, bf16[64,128]{1,0:T(8,128)(2,1)S(1)}, u32[]{:S(2)}, u32[]{:S(2)}) collective-permute-start(bf16[64,128]{1,0:T(8,128)(2,1)S(1)} %get-tuple-element.31), channel_id=1, source_target_pairs={{4,0},{6,2},{8,4},{10,6},{12,8},{14,10},{0,12},{2,14},{5,1},{7,3},... | collective-permute-start | bytes 49160 | tf_op jit(solution)/shard_map/ppermute | solution.py:379
  28.1 0.5 %collective-permute-start.7 = (bf16[64,256]{1,0:T(8,128)(2,1)S(1)}, bf16[64,256]{1,0:T(8,128)(2,1)S(1)}, u32[]{:S(2)}, u32[]{:S(2)}) collective-permute-start(bf16[64,256]{1,0:T(8,128)(2,1)S(1)} %bitcast.10), channel_id=1, source_target_pairs={{0,2},{2,0},{1,3},{3,1},{4,6},{6,4},{5,7},{7,5},{8,10},{10,8},{9,1... | collective-permute-start | bytes 98312 | tf_op jit(solution)/shard_map/ppermute | solution.py:382
  28.7 1.0 %collective-permute-done.6 = bf16[64,128]{1,0:T(8,128)(2,1)S(1)} collective-permute-done((bf16[64,128]{1,0:T(8,128)(2,1)S(1)}, bf16[64,128]{1,0:T(8,128)(2,1)S(1)}, u32[]{:S(2)}, u32[]{:S(2)}) %collective-permute-start.6) | collective-permute-done | bytes 16416 | tf_op jit(solution)/shard_map/ppermute | solution.py:379
  29.6 1.8 %collective-permute-done.5 = bf16[64,128]{1,0:T(8,128)(2,1)S(1)} collective-permute-done((bf16[64,128]{1,0:T(8,128)(2,1)S(1)}, bf16[64,128]{1,0:T(8,128)(2,1)S(1)}, u32[]{:S(2)}, u32[]{:S(2)}) %collective-permute-start.5) | collective-permute-done | bytes 16416 | tf_op jit(solution)/shard_map/ppermute | solution.py:379
  31.4 0.1 concatenate.10
  31.5 0.5 %collective-permute-done.7 = bf16[64,256]{1,0:T(8,128)(2,1)S(1)} collective-permute-done((bf16[64,256]{1,0:T(8,128)(2,1)S(1)}, bf16[64,256]{1,0:T(8,128)(2,1)S(1)}, u32[]{:S(2)}, u32[]{:S(2)}) %collective-permute-start.7) | collective-permute-done | bytes 32800 | tf_op jit(solution)/shard_map/ppermute | solution.py:382
  32.0 0.1 concatenate.12
  32.2 0.1 concatenate.11
  32.3 0.8 %fusion = bf16[64,3,2,64]{3,2,1,0:T(2,128)(2,1)} fusion(f32[64,1,2,64]{3,2,1,0:T(2,128)S(1)} %bitcast.12, f32[64,1,2,64]{3,2,1,0:T(2,128)S(1)} %bitcast.13, f32[64,1,2,64]{3,2,1,0:T(2,128)S(1)} %bitcast.11), kind=kLoop, calls=%fused_computation.1 | loop fusion | flops 98304 | bytes 147456 | tf_op jit(solution)/shard_map/convert_element_type | solution.py:386
  (4 shorter events, 0.0 us)
Async XLA Ops:
  3.9 18.1 %collective-permute-start.2 = (bf16[128,1024]{1,0:T(8,128)(2,1)S(1)}, bf16[128,1024]{1,0:T(8,128)(2,1)S(1)}, u32[]{:S(2)}, u32[]{:S(2)}) collective-permute-start(bf16[128,1024]{1,0:T(8,128)(2,1)S(1)} %get-tuple-element.20.refs_1_.refs_0_), channel_id=1, source_target_pairs={{0,4},{4,8},{8,12},{12,0},{1,5},{5,9},{9,13},{13,1},{2,6},{6,10},{... | collective-permute-start | bytes 786440 | tf_op jit(solution)/shard_map/ppermute | solution.py:305
  7.0 14.2 %collective-permute-start.3 = (bf16[64,1024]{1,0:T(8,128)(2,1)S(1)}, bf16[64,1024]{1,0:T(8,128)(2,1)S(1)}, u32[]{:S(2)}, u32[]{:S(2)}) collective-permute-start(bf16[64,1024]{1,0:T(8,128)(2,1)S(1)} %get-tuple-element.18.refs_0_), channel_id=1, source_target_pairs={{0,4},{4,8},{8,12},{12,0},{1,5},{5,9},{9,13},{13,1},{2,6},{6,10},{... | collective-permute-start | bytes 393224 | tf_op jit(solution)/shard_map/ppermute | solution.py:305
  8.6 2.3 %copy-start = (bf16[256,1024]{1,0:T(8,128)(2,1)S(1)}, bf16[256,1024]{1,0:T(8,128)(2,1)}, u32[]{:S(2)}) copy-start(bf16[256,1024]{1,0:T(8,128)(2,1)} %constant.7.clone.inv_ref.refs_0_) | copy-start | bytes 1572868
  9.2 13.6 %collective-permute-start.1 = (bf16[64,1024]{1,0:T(8,128)(2,1)S(1)}, bf16[64,1024]{1,0:T(8,128)(2,1)S(1)}, u32[]{:S(2)}, u32[]{:S(2)}) collective-permute-start(bf16[64,1024]{1,0:T(8,128)(2,1)S(1)} %shard_map.48.refs_2_.refs_3_), channel_id=1, source_target_pairs={{0,4},{4,8},{8,12},{12,0},{1,5},{5,9},{9,13},{13,1},{2,6},{6,10},{... | collective-permute-start | bytes 393224 | tf_op jit(solution)/shard_map/ppermute | solution.py:305
  10.8 10.2 %collective-permute-start = (s32[3,2,64]{2,1,0:T(2,128)S(1)}, s32[3,2,64]{2,1,0:T(2,128)S(1)}, u32[]{:S(2)}, u32[]{:S(2)}) collective-permute-start(s32[3,2,64]{2,1,0:T(2,128)S(1)} %get-tuple-element.17.vis_ref), channel_id=1, source_target_pairs={{0,4},{4,8},{8,12},{12,0},{1,5},{5,9},{9,13},{13,1},{2,6},{6,10},{... | collective-permute-start | bytes 4616 | tf_op jit(solution)/shard_map/ppermute | solution.py:306
  23.5 1.4 %collective-permute-start.4 = (bf16[128,384]{1,0:T(8,128)(2,1)S(1)}, bf16[128,384]{1,0:T(8,128)(2,1)S(1)}, u32[]{:S(2)}, u32[]{:S(2)}) collective-permute-start(bf16[128,384]{1,0:T(8,128)(2,1)S(1)} %bitcast.9), channel_id=1, source_target_pairs={{0,1},{1,0},{2,3},{3,2},{4,5},{5,4},{6,7},{7,6},{8,9},{9,8},{10,11... | collective-permute-start | bytes 294920 | tf_op jit(solution)/shard_map/ppermute | solution.py:353
  25.0 4.7 %collective-permute-start.6 = (bf16[64,128]{1,0:T(8,128)(2,1)S(1)}, bf16[64,128]{1,0:T(8,128)(2,1)S(1)}, u32[]{:S(2)}, u32[]{:S(2)}) collective-permute-start(bf16[64,128]{1,0:T(8,128)(2,1)S(1)} %get-tuple-element.32), channel_id=1, source_target_pairs={{4,2},{6,0},{8,6},{10,4},{12,10},{14,8},{0,14},{2,12},{5,3},{7,1},... | collective-permute-start | bytes 49160 | tf_op jit(solution)/shard_map/ppermute | solution.py:379
  27.7 3.7 %collective-permute-start.5 = (bf16[64,128]{1,0:T(8,128)(2,1)S(1)}, bf16[64,128]{1,0:T(8,128)(2,1)S(1)}, u32[]{:S(2)}, u32[]{:S(2)}) collective-permute-start(bf16[64,128]{1,0:T(8,128)(2,1)S(1)} %get-tuple-element.31), channel_id=1, source_target_pairs={{4,0},{6,2},{8,4},{10,6},{12,8},{14,10},{0,12},{2,14},{5,1},{7,3},... | collective-permute-start | bytes 49160 | tf_op jit(solution)/shard_map/ppermute | solution.py:379
  28.1 3.9 %collective-permute-start.7 = (bf16[64,256]{1,0:T(8,128)(2,1)S(1)}, bf16[64,256]{1,0:T(8,128)(2,1)S(1)}, u32[]{:S(2)}, u32[]{:S(2)}) collective-permute-start(bf16[64,256]{1,0:T(8,128)(2,1)S(1)} %bitcast.10), channel_id=1, source_target_pairs={{0,2},{2,0},{1,3},{3,1},{4,6},{6,4},{5,7},{7,5},{8,10},{10,8},{9,1... | collective-permute-start | bytes 98312 | tf_op jit(solution)/shard_map/ppermute | solution.py:382
